TPU v7x, 32 devices: a whole 2x2x4 slice. The times are simulated.
32 devices in a mesh: leaf: 8 (over y, x, core), seq: 4 (over z).
Axes of the slice: x: 2, y: 2, z: 4, core: 2. Of those that a mesh axis runs over, the one named last changes fastest.
Arguments:
- prompt_q: bfloat16 [8, 512, 1792], P('leaf', 'seq'), may hold values from -6 to 6
- prompt_k: bfloat16 [8, 512, 256], P('leaf', 'seq'), may hold values from -6 to 6
- prompt_value_rows: bfloat16 [8, 512, 256], P('leaf', 'seq'), may hold values from -6 to 6
- leaf_q: bfloat16 [8, 192, 1792], P('leaf', 'seq'), may hold values from -6 to 6
- leaf_k: bfloat16 [8, 192, 256], P('leaf', 'seq'), may hold values from -6 to 6
- leaf_value_rows: bfloat16 [8, 192, 256], P('leaf', 'seq'), may hold values from -6 to 6
- prompt_dy: bfloat16 [8, 512, 3584], P('leaf', 'seq'), may hold values from -6 to 6
- leaf_dy: bfloat16 [8, 192, 3584], P('leaf', 'seq'), may hold values from -6 to 6
- out_weight: bfloat16 [1792, 3584], replicated, may hold values from -0.125 to 0.125
- lengths: int32 [8, 16], P('leaf'), may hold values from 1 to 24, 192 in all within a row
- offsets: int32 [8, 16], P('leaf'), may hold values from 1 to 512
- parents: int32 [8, 16], P('leaf'), may hold values from 0 to 15, as said below
Outputs:
- prompt_dq: float32 [8, 512, 1792], P('leaf', 'seq')
- prompt_dk: float32 [8, 512, 256], P('leaf', 'seq')
- prompt_dv: float32 [8, 512, 256], P('leaf', 'seq')
- leaf_dq: float32 [8, 192, 1792], P('leaf', 'seq')
- leaf_dk: float32 [8, 192, 256], P('leaf', 'seq')
- leaf_dv: float32 [8, 192, 256], P('leaf', 'seq')
- weight_grad: float32 [1792, 3584], P(('leaf', 'seq'))
Inputs may be any that keep to these rules, and one draw needn't show every extreme that they name: parents[t, b] lies in 0 to b; the value b means that branch b has no ancestor branch.
All inputs are finite; a program needn't handle non-finite values.
Results may differ from a plain program's by a relative error of at most 0.025.
Values may be sent and summed in bfloat16 or wider, within the bound.
No kernel may reach another device: no remote copies, remote signals or barrier semaphores. Data moves between devices by JAX's collectives and lax.ppermute only.
A program may use at most 128 MiB of HBM per device.

v0:
```python
import math
import jax
import jax.numpy as jnp
from jax import lax
from jax.sharding import PartitionSpec as P

HEAD_SIZE = 128
QUERY_HEADS = 14
KEY_VALUE_HEADS = 2
QUERY_PER_KV = 7


def leaf_visibility(lengths, offsets, parents, query_index, prompt_total, leaf_total):
    branch_ends = jnp.cumsum(lengths)
    branch_ids = jnp.arange(lengths.shape[0], dtype=jnp.int32)
    leaf_index = jnp.arange(leaf_total, dtype=jnp.int32)
    key_branch = jnp.sum((leaf_index[:, None] >= branch_ends[None, :]).astype(jnp.int32), axis=1)
    query_branch = jnp.sum((query_index[:, None] >= branch_ends[None, :]).astype(jnp.int32), axis=1)
    member = (query_branch[:, None] == branch_ids[None, :]).astype(jnp.int32)
    fork_point = jnp.sum(member * offsets[None, :], axis=1)
    ancestor = jnp.sum(member * parents[None, :], axis=1)
    prompt_index = jnp.arange(prompt_total, dtype=jnp.int32)
    sees_prompt = prompt_index[None, :] < fork_point[:, None]
    own_branch = (key_branch[None, :] == query_branch[:, None]) & (
        leaf_index[None, :] <= query_index[:, None]
    )
    inherited = (key_branch[None, :] == ancestor[:, None]) & (
        ancestor[:, None] != query_branch[:, None]
    )
    return jnp.concatenate([sees_prompt, own_branch | inherited], axis=1)


def weight_gradient(attn_out, upstream, tree_count, seq_count):
    width_total = attn_out.shape[1]
    device_rows = attn_out.shape[0]
    row_share = width_total // (tree_count * seq_count)
    normalizer = 1.0 / math.sqrt(tree_count * seq_count * device_rows)
    parted = attn_out.reshape(device_rows, tree_count, seq_count, row_share)
    moved = lax.all_to_all(parted, "seq", split_axis=2, concat_axis=0, tiled=True)
    picked = moved.reshape(device_rows * seq_count, tree_count * row_share)
    tree_grad = lax.all_gather(upstream, "seq", axis=0, tiled=True)
    partial_term = lax.dot_general(
        picked, tree_grad, (((0,), (0,)), ((), ())), preferred_element_type=jnp.float32
    )
    summed = lax.psum_scatter(
        partial_term.astype(jnp.bfloat16), "leaf", scatter_dimension=0, tiled=True
    ).astype(jnp.float32)
    return summed * normalizer


def body(
    prompt_q,
    prompt_k,
    prompt_value_rows,
    leaf_q,
    leaf_k,
    leaf_value_rows,
    prompt_dy,
    leaf_dy,
    out_weight,
    lengths,
    offsets,
    parents,
):
    seq_count = lax.axis_size("seq")
    tree_count = lax.axis_size("leaf")
    seq_index = lax.axis_index("seq")
    prompt_dev = prompt_q.shape[1]
    leaf_dev = leaf_q.shape[1]
    device_rows = prompt_dev + leaf_dev
    prompt_total = prompt_dev * seq_count
    leaf_total = leaf_dev * seq_count
    score_scale = 1.0 / math.sqrt(HEAD_SIZE)
    gathered = (
        lax.all_gather(prompt_k, "seq", axis=1, tiled=True),
        lax.all_gather(prompt_value_rows, "seq", axis=1, tiled=True),
        lax.all_gather(leaf_k, "seq", axis=1, tiled=True),
        lax.all_gather(leaf_value_rows, "seq", axis=1, tiled=True),
    )
    key_rows = jnp.concatenate([gathered[0][0], gathered[2][0]], axis=0)
    value_rows = jnp.concatenate([gathered[1][0], gathered[3][0]], axis=0)
    query_rows = jnp.concatenate([prompt_q[0], leaf_q[0]], axis=0)
    upstream = jnp.concatenate([prompt_dy[0], leaf_dy[0]], axis=0)
    prompt_index = seq_index * prompt_dev + jnp.arange(prompt_dev, dtype=jnp.int32)
    leaf_index = seq_index * leaf_dev + jnp.arange(leaf_dev, dtype=jnp.int32)
    prompt_keys = jnp.arange(prompt_total, dtype=jnp.int32)
    prompt_sees = jnp.concatenate(
        [
            prompt_keys[None, :] <= prompt_index[:, None],
            jnp.zeros((prompt_dev, leaf_total), dtype=jnp.bool_),
        ],
        axis=1,
    )
    leaf_sees = leaf_visibility(
        lengths[0], offsets[0], parents[0], leaf_index, prompt_total, leaf_total
    )
    visible = jnp.concatenate([prompt_sees, leaf_sees], axis=0)
    grouped_queries = query_rows.reshape(device_rows, KEY_VALUE_HEADS, QUERY_PER_KV, HEAD_SIZE)
    output_gradient = lax.dot_general(
        upstream, out_weight, (((1,), (1,)), ((), ())), preferred_element_type=jnp.float32
    ).astype(jnp.bfloat16)
    gradient_groups = output_gradient.reshape(device_rows, KEY_VALUE_HEADS, QUERY_PER_KV, HEAD_SIZE)
    prob_list, weight_list, attn_list = ([], [], [])
    for key_value_group in range(KEY_VALUE_HEADS):
        key_block = key_rows[:, key_value_group * HEAD_SIZE : (key_value_group + 1) * HEAD_SIZE]
        value_block = value_rows[:, key_value_group * HEAD_SIZE : (key_value_group + 1) * HEAD_SIZE]
        scores = (
            jnp.einsum(
                "qhd,kd->hqk",
                grouped_queries[:, key_value_group],
                key_block,
                preferred_element_type=jnp.float32,
            )
            * score_scale
        )
        scores = jnp.where(visible[None], scores, -jnp.inf)
        shifted = jnp.exp(scores - jnp.max(scores, axis=2, keepdims=True))
        probabilities = shifted / jnp.sum(shifted, axis=2, keepdims=True)
        weights = probabilities.astype(jnp.bfloat16)
        attn_list.append(
            jnp.einsum(
                "hqk,kd->qhd", weights, value_block, preferred_element_type=jnp.float32
            ).astype(jnp.bfloat16)
        )
        prob_list.append(probabilities)
        weight_list.append(weights)
    attn_out = jnp.stack(attn_list, axis=1).reshape(device_rows, QUERY_HEADS * HEAD_SIZE)
    dscore_list, dq_list = ([], [])
    for key_value_group in range(KEY_VALUE_HEADS):
        key_block = key_rows[:, key_value_group * HEAD_SIZE : (key_value_group + 1) * HEAD_SIZE]
        value_block = value_rows[:, key_value_group * HEAD_SIZE : (key_value_group + 1) * HEAD_SIZE]
        row_dot = jnp.sum(
            gradient_groups[:, key_value_group].astype(jnp.float32)
            * attn_list[key_value_group].astype(jnp.float32),
            axis=2,
        )
        prob_grad = jnp.einsum(
            "qhd,kd->hqk",
            gradient_groups[:, key_value_group],
            value_block,
            preferred_element_type=jnp.float32,
        )
        dscore = (
            prob_list[key_value_group] * (prob_grad - row_dot.T[:, :, None]) * score_scale
        ).astype(jnp.bfloat16)
        dq_list.append(
            jnp.einsum("hqk,kd->qhd", dscore, key_block, preferred_element_type=jnp.float32)
        )
        dscore_list.append(dscore)
    query_grad = jnp.stack(dq_list, axis=1).reshape(device_rows, QUERY_HEADS * HEAD_SIZE)
    first_block = jnp.int32(0) // device_rows
    blocks = device_rows * lax.axis_size("seq") // device_rows
    prompt_cols = blocks * prompt_dev
    leaf_cols = blocks * leaf_dev
    key_parts = []
    value_parts = []
    for key_value_group in range(KEY_VALUE_HEADS):
        picked_d = jnp.concatenate(
            [
                lax.dynamic_slice_in_dim(
                    dscore_list[key_value_group], first_block * prompt_dev, prompt_cols, 2
                ),
                lax.dynamic_slice_in_dim(dscore_list[key_value_group], prompt_total, leaf_cols, 2),
            ],
            axis=2,
        )
        picked_w = jnp.concatenate(
            [
                lax.dynamic_slice_in_dim(
                    weight_list[key_value_group], first_block * prompt_dev, prompt_cols, 2
                ),
                lax.dynamic_slice_in_dim(weight_list[key_value_group], prompt_total, leaf_cols, 2),
            ],
            axis=2,
        )
        key_parts.append(
            jnp.einsum(
                "hqk,qhd->kd",
                picked_d,
                grouped_queries[:, key_value_group],
                preferred_element_type=jnp.float32,
            )
        )
        value_parts.append(
            jnp.einsum(
                "hqk,qhd->kd",
                picked_w,
                gradient_groups[:, key_value_group],
                preferred_element_type=jnp.float32,
            )
        )
    joined = jnp.concatenate(key_parts + value_parts, axis=1)
    stacked_width = joined.shape[1]
    prompt_part = joined[:prompt_cols].reshape(blocks, prompt_dev, stacked_width)
    leaf_part = joined[prompt_cols:].reshape(blocks, leaf_dev, stacked_width)
    key_grads = lax.psum_scatter(
        jnp.concatenate([prompt_part, leaf_part], axis=1)
        .reshape(device_rows * lax.axis_size("seq"), stacked_width)
        .astype(jnp.bfloat16),
        "seq",
        scatter_dimension=0,
        tiled=True,
    ).astype(jnp.float32)
    weight_grad = weight_gradient(attn_out, upstream, tree_count, seq_count)
    key_value_width = KEY_VALUE_HEADS * HEAD_SIZE
    return (
        query_grad[:prompt_dev][None],
        key_grads[:prompt_dev, :key_value_width][None],
        key_grads[:prompt_dev, key_value_width:][None],
        query_grad[prompt_dev:][None],
        key_grads[prompt_dev:, :key_value_width][None],
        key_grads[prompt_dev:, key_value_width:][None],
        weight_grad,
    )


def solution(mesh):
    placed = (
        P("leaf", "seq", None),
        P("leaf", "seq", None),
        P("leaf", "seq", None),
        P("leaf", "seq", None),
        P("leaf", "seq", None),
        P("leaf", "seq", None),
        P("leaf", "seq", None),
        P("leaf", "seq", None),
        P(),
        P("leaf", None),
        P("leaf", None),
        P("leaf", None),
    )
    return jax.shard_map(
        body,
        mesh=mesh,
        in_specs=placed,
        out_specs=(
            P("leaf", "seq", None),
            P("leaf", "seq", None),
            P("leaf", "seq", None),
            P("leaf", "seq", None),
            P("leaf", "seq", None),
            P("leaf", "seq", None),
            P(("leaf", "seq"), None),
        ),
        check_vma=False,
    )
```

profile of v0, /device:TPU:0, one launch (start us, length us, event | category | flops | bytes accessed | tf_op | source)
XLA Modules:
  0.0 209.9 jit_solution(18198870469097177820)
XLA Ops:
  7.3 2.5 %pad_maximum_fusion = bf16[176,3584]{1,0:T(8,128)(2,1)} fusion(bf16[48,3584]{1,0:T(8,128)(2,1)} %bitcast.198, bf16[128,3584]{1,0:T(8,128)(2,1)} %bitcast.187), kind=kLoop, calls=%fused_computation.31 | loop fusion | flops 2523136 | bytes 2523136 | tf_op jit(solution)/shard_map/concatenate | solution.py:83
  11.8 9.1 %convolution_convert_fusion.1 = bf16[176,1792]{1,0:T(8,128)(2,1)S(1)} fusion(bf16[1792,3584]{1,0:T(8,128)(2,1)} %param.20, bf16[48,3584]{1,0:T(8,128)(2,1)S(1)} %bitcast.199, bf16[128,3584]{1,0:T(8,128)(2,1)S(1)} %bitcast.188), kind=kOutput, calls=%fused_computation.17 | convolution fusion | flops 2263568384 | bytes 14737408 | tf_op jit(solution)/shard_map/dot_general | solution.py:99
  20.9 0.7 reshape.92
  21.7 16.0 %all_gather.16 = bf16[1,192,256]{2,1,0:T(8,128)(2,1)S(1)} all-gather(bf16[1,48,256]{2,1,0:T(8,128)(2,1)S(1)} %copy-done.27), channel_id=1, replica_groups=mesh['leaf'=8,'seq'=4] {'seq'}, dimensions={1}, use_global_device_ids=true | all-gather | bytes 122880 | tf_op jit(solution)/shard_map/all_gather | solution.py:77
  37.6 15.0 %all_gather.18 = bf16[1,192,256]{2,1,0:T(8,128)(2,1)S(1)} all-gather(bf16[1,48,256]{2,1,0:T(8,128)(2,1)S(1)} %copy-done.28), channel_id=1, replica_groups=mesh['leaf'=8,'seq'=4] {'seq'}, dimensions={1}, use_global_device_ids=true | all-gather | bytes 122880 | tf_op jit(solution)/shard_map/all_gather | solution.py:78
  52.7 18.1 %all_gather.15 = bf16[1,512,256]{2,1,0:T(8,128)(2,1)S(1)} all-gather(bf16[1,128,256]{2,1,0:T(8,128)(2,1)S(1)} %copy-done.26), channel_id=1, replica_groups=mesh['leaf'=8,'seq'=4] {'seq'}, dimensions={1}, use_global_device_ids=true | all-gather | bytes 327680 | tf_op jit(solution)/shard_map/all_gather | solution.py:75
  70.7 17.5 %all_gather.17 = bf16[1,512,256]{2,1,0:T(8,128)(2,1)S(1)} all-gather(bf16[1,128,256]{2,1,0:T(8,128)(2,1)} %param.14), channel_id=1, replica_groups=mesh['leaf'=8,'seq'=4] {'seq'}, dimensions={1}, use_global_device_ids=true | all-gather | bytes 327680 | tf_op jit(solution)/shard_map/all_gather | solution.py:76
  88.7 0.9 fusion.66
  89.6 3.3 %fusion.76 = (f32[7,176]{1,0:T(8,128)S(1)}, f32[7,176,704]{2,1,0:T(8,128)}) fusion(pred[176,704]{1,0:T(8,128)(4,1)S(1)} %pad_add_fusion, bf16[192,256]{1,0:T(8,128)(2,1)S(1)} %bitcast.189, bf16[512,256]{1,0:T(8,128)(2,1)S(1)} %bitcast.175, bf16[48,2,7,128]{3,0,2,1:T(8,128)(2,1)S(1)} %copy-done.24, bf16[128,2,7,128]{3,0,2,1:T(8,128)(2,1)S(1)} %copy.47), kind=kOutput, calls=%fused_computation.98 | convolution fusion | flops 226497216 | bytes 4589376 | tf_op jit(solution)/shard_map/sub | solution.py:117
  93.0 2.4 %fusion.17 = bf16[7,176,704]{2,1,0:T(8,128)(2,1)S(1)} fusion(f32[7,176,704]{2,1,0:T(8,128)} %get-tuple-element.41, f32[7,176]{1,0:T(8,128)S(1)} %get-tuple-element.40), kind=kLoop, calls=%fused_computation.27 | loop fusion | flops 1734656 | bytes 5208896 | tf_op jit(solution)/shard_map/convert_element_type | solution.py:119
  95.4 1.4 multiply_reduce_fusion
  96.8 4.3 %fusion.67 = (f32[7,176]{1,0:T(8,128)S(1)}, f32[7,176,704]{2,1,0:T(8,128)}) fusion(pred[176,704]{1,0:T(8,128)(4,1)S(1)} %pad_add_fusion, bf16[512,256]{1,0:T(8,128)(2,1)S(1)} %bitcast.176, bf16[192,256]{1,0:T(8,128)(2,1)S(1)} %bitcast.190, bf16[128,2,7,128]{3,0,2,1:T(8,128)(2,1)S(1)} %copy-done.20, bf16[48,2,7,128]{3,0,2,1:T(8,128)(2,1)} %copy.48), kind=kOutput, calls=%fused_computation.97 | convolution fusion | flops 226497216 | bytes 4589376 | tf_op jit(solution)/shard_map/sub | solution.py:117
  101.1 2.4 %fusion.16 = bf16[7,176,704]{2,1,0:T(8,128)(2,1)S(1)} fusion(f32[7,176,704]{2,1,0:T(8,128)} %get-tuple-element.37, f32[7,176]{1,0:T(8,128)S(1)} %get-tuple-element.36), kind=kLoop, calls=%fused_computation.26 | loop fusion | flops 1734656 | bytes 5208896 | tf_op jit(solution)/shard_map/convert_element_type | solution.py:119
  103.6 1.2 copy-done
  104.8 1.4 multiply_reduce_fusion.1
  106.7 1.0 copy.54
  107.7 5.6 %all-to-all-start = ((bf16[176,8,4,56]{0,3,1,2:T(8,128)(2,1)}), bf16[176,8,4,56]{0,3,1,2:T(8,128)(2,1)S(1)}, u32[]{:S(2)}, u32[]{:S(2)}) async-start(bf16[176,8,4,56]{0,3,1,2:T(8,128)(2,1)} %copy.54), calls=%async_computation.1 | async-start | bytes 1835008 | tf_op jit(solution)/shard_map/all_to_all | solution.py:39
  113.3 2.7 %fusion.4 = bf16[7,176,704]{2,1,0:T(8,128)(2,1)S(1)} fusion(f32[7,176]{1,0:T(8,128)S(1)} %bitcast.201, f32[7,176,704]{2,1,0:T(8,128)} %get-tuple-element.41, f32[7,176]{1,0:T(8,128)S(1)} %get-tuple-element.40, bf16[176,1,7,128]{3,2,1,0:T(8,128)(2,1)S(1)} %copy-done.14, bf16[192,256]{1,0:T(8,128)(2,1)} %bitcast.195, bf16[512,256]{1,0:T(8,128)(2,1)S(1)} %bitcast.181), kind=kOutput, calls=%fused_computation.6 | convolution fusion | flops 226733056 | bytes 5889664 | tf_op jit(solution)/shard_map/qhd,kd->hqk/dot_general | solution.py:137
  116.0 1.3 copy-done.7
  120.3 1.1 fusion.7
  121.4 0.7 convolution_bitcast_fusion.5
  122.7 0.9 pad_maximum_fusion.1
  123.7 22.3 %all-to-all-done = bf16[176,8,4,56]{0,3,1,2:T(8,128)(2,1)S(1)} async-done(((bf16[176,8,4,56]{0,3,1,2:T(8,128)(2,1)}), bf16[176,8,4,56]{0,3,1,2:T(8,128)(2,1)S(1)}, u32[]{:S(2)}, u32[]{:S(2)}) %all-to-all-start) | async-done | bytes 630816 | tf_op jit(solution)/shard_map/all_to_all | solution.py:39
  146.7 0.7 reshape.95
  147.5 6.5 %convolution_convert_fusion = bf16[448,3584]{1,0:T(8,128)(2,1)} fusion(bf16[704,448]{0,1:T(8,128)(2,1)S(1)} %reshape.95, bf16[704,3584]{1,0:T(8,128)(2,1)} %all-gather.2.cloned.1.call-done), kind=kOutput, calls=%fused_computation.2 | convolution fusion | flops 2262335488 | bytes 8888320 | tf_op jit(solution)/shard_map/dot_general | solution.py:42
  154.0 0.9 copy-done.4
  156.3 0.9 copy-done.10
  158.2 1.2 copy.56
  159.6 0.8 broadcast_in_dim.33
  160.4 0.9 convert_element_type.75
  162.7 38.7 %reduce-scatter.5.cloned.1.call-done = bf16[56,3584]{1,0:T(8,128)(2,1)} async-done(((bf16[448,3584]{1,0:T(8,128)(2,1)}), bf16[56,3584]{1,0:T(8,128)(2,1)}) %reduce-scatter.5.cloned.1.call-update) | async-done | bytes 401424 | tf_op jit(solution)/shard_map/reduce_scatter | solution.py:45
  201.5 1.9 convert_multiply_fusion
  (106 shorter events, 11.0 us)
Async XLA Ops:
  7.2 2.6 %copy-start.31 = (s32[1,16]{1,0:T(1,128)S(1)}, s32[1,16]{1,0:T(1,128)}, u32[]{:S(2)}) copy-start(s32[1,16]{1,0:T(1,128)} %param.21) | copy-start | bytes 196
  7.2 3.0 %copy-start.33 = (s32[1,16]{1,0:T(1,128)S(1)}, s32[1,16]{1,0:T(1,128)}, u32[]{:S(2)}) copy-start(s32[1,16]{1,0:T(1,128)} %param.23) | copy-start | bytes 196
  7.2 3.0 %copy-start.32 = (s32[1,16]{1,0:T(1,128)S(1)}, s32[1,16]{1,0:T(1,128)}, u32[]{:S(2)}) copy-start(s32[1,16]{1,0:T(1,128)} %param.22) | copy-start | bytes 196
  7.2 3.1 %copy-start.23 = (bf16[1,48,1792]{2,1,0:T(8,128)(2,1)S(1)}, bf16[1,48,1792]{2,1,0:T(8,128)(2,1)}, u32[]{:S(2)}) copy-start(bf16[1,48,1792]{2,1,0:T(8,128)(2,1)} %param.15) | copy-start | bytes 516100
  7.2 4.0 %copy-start.18 = (bf16[1,128,1792]{2,1,0:T(8,128)(2,1)S(1)}, bf16[1,128,1792]{2,1,0:T(8,128)(2,1)}, u32[]{:S(2)}) copy-start(bf16[1,128,1792]{2,1,0:T(8,128)(2,1)} %param.12) | copy-start | bytes 1376260
  7.2 140.3 %all-gather.2.cloned.1.call-start = ((), (), s32[]{:S(2)}) async-start(), calls=%async_computation.4 | async-start | bytes 6307840 | tf_op jit(solution)/shard_map/all_gather | solution.py:41
  9.8 2.0 copy-start.15
  9.8 2.0 copy-start.22
  11.7 77.9 %copy-start.19 = (bf16[128,2,7,128]{3,0,2,1:T(8,128)(2,1)}, bf16[128,2,7,128]{3,0,2,1:T(8,128)(2,1)S(1)}, u32[]{:S(2)}) copy-start(bf16[128,2,7,128]{3,0,2,1:T(8,128)(2,1)S(1)} %copy.47) | copy-start | bytes 1376260
  11.8 9.9 %copy-start.27 = (bf16[1,48,256]{2,1,0:T(8,128)(2,1)S(1)}, bf16[1,48,256]{2,1,0:T(8,128)(2,1)}, u32[]{:S(2)}) copy-start(bf16[1,48,256]{2,1,0:T(8,128)(2,1)} %param.16) | copy-start | bytes 73732
  11.8 25.9 %copy-start.28 = (bf16[1,48,256]{2,1,0:T(8,128)(2,1)S(1)}, bf16[1,48,256]{2,1,0:T(8,128)(2,1)}, u32[]{:S(2)}) copy-start(bf16[1,48,256]{2,1,0:T(8,128)(2,1)} %param.17) | copy-start | bytes 73732
  11.8 40.9 %copy-start.26 = (bf16[1,128,256]{2,1,0:T(8,128)(2,1)S(1)}, bf16[1,128,256]{2,1,0:T(8,128)(2,1)}, u32[]{:S(2)}) copy-start(bf16[1,128,256]{2,1,0:T(8,128)(2,1)} %param.13) | copy-start | bytes 196612
  20.9 68.7 %copy-start.24 = (bf16[48,2,7,128]{3,0,2,1:T(8,128)(2,1)S(1)}, bf16[48,2,7,128]{3,0,2,1:T(8,128)(2,1)}, u32[]{:S(2)}) copy-start(bf16[48,2,7,128]{3,0,2,1:T(8,128)(2,1)} %copy.48) | copy-start | bytes 516100
  52.7 50.9 %copy-start.16 = (bf16[1,192,256]{2,1,0:T(8,128)(2,1)}, bf16[1,192,256]{2,1,0:T(8,128)(2,1)S(1)}, u32[]{:S(2)}) copy-start(bf16[1,192,256]{2,1,0:T(8,128)(2,1)S(1)} %all_gather.18) | copy-start | bytes 294916
  70.7 26.1 %copy-start.3 = (bf16[1,512,256]{2,1,0:T(8,128)(2,1)}, bf16[1,512,256]{2,1,0:T(8,128)(2,1)S(1)}, u32[]{:S(2)}) copy-start(bf16[1,512,256]{2,1,0:T(8,128)(2,1)S(1)} %all_gather.15) | copy-start | bytes 786436
  88.3 15.3 %copy-start.5 = (bf16[1,512,256]{2,1,0:T(8,128)(2,1)}, bf16[1,512,256]{2,1,0:T(8,128)(2,1)S(1)}, u32[]{:S(2)}) copy-start(bf16[1,512,256]{2,1,0:T(8,128)(2,1)S(1)} %all_gather.17) | copy-start | bytes 786436
  93.0 2.5 %copy-start.13 = (bf16[176,1,7,128]{3,2,1,0:T(8,128)(2,1)S(1)}, bf16[176,1,7,128]{3,2,1,0:T(8,128)(2,1)}, u32[]{:S(2)}) copy-start(bf16[176,1,7,128]{3,2,1,0:T(8,128)(2,1)} %get-tuple-element.30) | copy-start | bytes 946180
  101.1 3.7 %copy-start.11 = (bf16[176,1,7,128]{3,2,1,0:T(8,128)(2,1)S(1)}, bf16[176,1,7,128]{3,2,1,0:T(8,128)(2,1)}, u32[]{:S(2)}) copy-start(bf16[176,1,7,128]{3,2,1,0:T(8,128)(2,1)} %get-tuple-element.31) | copy-start | bytes 946180
  106.6 6.6 %copy-start.6 = (bf16[1,512,256]{2,1,0:T(8,128)(2,1)S(1)}, bf16[1,512,256]{2,1,0:T(8,128)(2,1)}, u32[]{:S(2)}) copy-start(bf16[1,512,256]{2,1,0:T(8,128)(2,1)} %copy-done.5) | copy-start | bytes 786436
  106.6 6.6 %copy-start.14 = (bf16[176,1,7,128]{3,2,1,0:T(8,128)(2,1)S(1)}, bf16[176,1,7,128]{3,2,1,0:T(8,128)(2,1)}, u32[]{:S(2)}) copy-start(bf16[176,1,7,128]{3,2,1,0:T(8,128)(2,1)} %get-tuple-element.30) | copy-start | bytes 946180
  106.7 6.6 %copy-start.30 = (f32[176,7]{0,1:T(8,128)S(1)}, f32[176,7]{0,1:T(8,128)}, u32[]{:S(2)}) copy-start(f32[176,7]{0,1:T(8,128)} %get-tuple-element.42) | copy-start | bytes 14788
  107.7 38.4 %all-to-all-start = ((bf16[176,8,4,56]{0,3,1,2:T(8,128)(2,1)}), bf16[176,8,4,56]{0,3,1,2:T(8,128)(2,1)S(1)}, u32[]{:S(2)}, u32[]{:S(2)}) async-start(bf16[176,8,4,56]{0,3,1,2:T(8,128)(2,1)} %copy.54), calls=%async_computation.1 | async-start | bytes 1835008 | tf_op jit(solution)/shard_map/all_to_all | solution.py:39
  113.2 47.2 %reduce-scatter.3.cloned.1.call-start = ((), (), s32[]{:S(2)}) async-start(), calls=%async_computation.3 | async-start | bytes 901120 | tf_op jit(solution)/shard_map/reduce_scatter | solution.py:196
  113.2 4.1 %copy-start.21 = (bf16[128,2,7,128]{3,0,2,1:T(8,128)(2,1)S(1)}, bf16[128,2,7,128]{3,0,2,1:T(8,128)(2,1)}, u32[]{:S(2)}) copy-start(bf16[128,2,7,128]{3,0,2,1:T(8,128)(2,1)} %copy-done.19) | copy-start | bytes 1376260
  113.2 4.1 %copy-start.25 = (bf16[48,2,7,128]{3,0,2,1:T(8,128)(2,1)S(1)}, bf16[48,2,7,128]{3,0,2,1:T(8,128)(2,1)}, u32[]{:S(2)}) copy-start(bf16[48,2,7,128]{3,0,2,1:T(8,128)(2,1)} %copy.48) | copy-start | bytes 516100
  117.3 1.5 copy-start.1
  117.3 1.6 copy-start.12
  118.1 2.2 %copy-start.2 = (f32[7,176,704]{2,1,0:T(8,128)S(1)}, f32[7,176,704]{2,1,0:T(8,128)}, u32[]{:S(2)}) copy-start(f32[7,176,704]{2,1,0:T(8,128)} %get-tuple-element.37) | copy-start | bytes 10407940
  118.1 2.2 %copy-start.17 = (bf16[1,192,256]{2,1,0:T(8,128)(2,1)S(1)}, bf16[1,192,256]{2,1,0:T(8,128)(2,1)}, u32[]{:S(2)}) copy-start(bf16[1,192,256]{2,1,0:T(8,128)(2,1)} %copy-done.16) | copy-start | bytes 294916
  118.1 2.2 %copy-start.29 = (f32[176,7]{0,1:T(8,128)S(1)}, f32[176,7]{0,1:T(8,128)}, u32[]{:S(2)}) copy-start(f32[176,7]{0,1:T(8,128)} %get-tuple-element.38) | copy-start | bytes 14788
  123.7 77.8 %reduce-scatter.5.cloned.1.call-start = ((), (), s32[]{:S(2)}) async-start(), calls=%async_computation.5 | async-start | bytes 3612672 | tf_op jit(solution)/shard_map/reduce_scatter | solution.py:45
  154.0 1.6 copy-start.8
  (6 other events, 7.8 us)
Sparse Core Ops, SparseCore 0:
  9.9 115.1 all-gather.1
  128.0 22.7 reduce-scatter.2
  154.2 47.1 reduce-scatter.4
where the time goes:
time: 210 us
  blocking collectives  66.6 us (32%)
  waiting for transfers between devices  61.1 us (29%)
  matrix products  34.1 us (16%)
  local copies, waits for them, and re-layouts  16.1 us (8%)
  between operations  14.2 us (7%)
  other arithmetic  12.2 us (6%)
  starting transfers between devices  5.63 us (3%)
    reduce_scatter x1, waiting for transfers between devices, weight_gradient(): lax.psum_scatter(partial_term.astype(jnp.bfloat16), 'leaf', scatter_dimen...  38.7 us
    all_to_all x1, waiting for transfers between devices, weight_gradient(): lax.all_to_all(parted, 'seq', split_axis=2, concat_axis=0, tiled=True)  22.3 us
    all_gather x1, blocking collectives, body(): lax.all_gather(prompt_k, 'seq', axis=1, tiled=True)  18.1 us
    all_gather x1, blocking collectives, body(): lax.all_gather(prompt_value_rows, 'seq', axis=1, tiled=True)  17.5 us
    all_gather x1, blocking collectives, body(): lax.all_gather(leaf_k, 'seq', axis=1, tiled=True)  16 us
    all_gather x1, blocking collectives, body(): lax.all_gather(leaf_value_rows, 'seq', axis=1, tiled=True)  15 us
    dot_general x1, matrix products, body(): lax.dot_general(upstream, out_weight, (((1,), (1,)), ((), ())), preferred...  9.1 us
    unnamed x70, local copies, waits for them, and re-layouts  7.78 us
  transfers between devices with their start and end apart: 4, of which 2 were waited for; matrix products, arithmetic and copies ran while one was open for 25% of the time, Pallas kernels for 0%

commit v1 on v0

--- a/solution.py
+++ b/solution.py
@@ -36,7 +36,10 @@
     row_share = width_total // (tree_count * seq_count)
     normalizer = 1.0 / math.sqrt(tree_count * seq_count * device_rows)
     parted = attn_out.reshape(device_rows, tree_count, seq_count, row_share)
-    moved = lax.all_to_all(parted, "seq", split_axis=2, concat_axis=0, tiled=True)
+    moved = jnp.concatenate(
+        lax.all_to_all(jnp.stack(jnp.split(parted, lax.axis_size("seq"), axis=2)), "seq", 0, 0),
+        axis=0,
+    )
     picked = moved.reshape(device_rows * seq_count, tree_count * row_share)
     tree_grad = lax.all_gather(upstream, "seq", axis=0, tiled=True)
     partial_term = lax.dot_general(

time: 210 us -> 210 us (level)
    unnamed x70 -> x76, local copies, waits for them, and re-layouts: 7.78 us -> 7.72 us
where the time goes in v1:
time: 210 us
  blocking collectives  66.2 us (32%)
  waiting for transfers between devices  61 us (29%)
  matrix products  34.7 us (17%)
  local copies, waits for them, and re-layouts  15 us (7%)
  between operations  14.3 us (7%)
  other arithmetic  13.3 us (6%)
  starting transfers between devices  5.52 us (3%)
    reduce_scatter x1, waiting for transfers between devices, weight_gradient(): lax.psum_scatter(partial_term.astype(jnp.bfloat16), 'leaf', scatter_dimen...  38.8 us
    all_to_all x1, waiting for transfers between devices, weight_gradient(): lax.all_to_all(jnp.stack(jnp.split(parted, lax.axis_size('seq'), axis=2))...  22.1 us
    all_gather x1, blocking collectives, body(): lax.all_gather(prompt_k, 'seq', axis=1, tiled=True)  18.1 us
    all_gather x1, blocking collectives, body(): lax.all_gather(prompt_value_rows, 'seq', axis=1, tiled=True)  17.8 us
    all_gather x1, blocking collectives, body(): lax.all_gather(leaf_k, 'seq', axis=1, tiled=True)  16 us
    all_gather x1, blocking collectives, body(): lax.all_gather(leaf_value_rows, 'seq', axis=1, tiled=True)  14.4 us
    dot_general x1, matrix products, body(): lax.dot_general(upstream, out_weight, (((1,), (1,)), ((), ())), preferred...  8.98 us
    sub x2, matrix products, body(): shifted = jnp.exp(scores - jnp.max(scores, axis=2, keepdims=True))  7.74 us
  transfers between devices with their start and end apart: 4, of which 2 were waited for; matrix products, arithmetic and copies ran while one was open for 25% of the time, Pallas kernels for 0%

profile of v1, /device:TPU:0, one launch (start us, length us, event | category | flops | bytes accessed | tf_op | source)
XLA Modules:
  0.0 209.9 jit_solution(6407642861152149729)
XLA Ops:
  7.3 2.5 %pad_maximum_fusion = bf16[176,3584]{1,0:T(8,128)(2,1)} fusion(bf16[48,3584]{1,0:T(8,128)(2,1)} %bitcast.208, bf16[128,3584]{1,0:T(8,128)(2,1)} %bitcast.197), kind=kLoop, calls=%fused_computation.31 | loop fusion | flops 2523136 | bytes 2523136 | tf_op jit(solution)/shard_map/concatenate | solution.py:86
  11.5 1.0 copy.41
  12.5 9.0 %convolution_convert_fusion.1 = bf16[176,1792]{1,0:T(8,128)(2,1)S(1)} fusion(bf16[1792,3584]{1,0:T(8,128)(2,1)} %param.20, bf16[48,3584]{1,0:T(8,128)(2,1)S(1)} %bitcast.209, bf16[128,3584]{1,0:T(8,128)(2,1)S(1)} %bitcast.198), kind=kOutput, calls=%fused_computation.17 | convolution fusion | flops 2263568384 | bytes 14737408 | tf_op jit(solution)/shard_map/dot_general | solution.py:102
  22.3 16.0 %all_gather.16 = bf16[1,192,256]{2,1,0:T(8,128)(2,1)S(1)} all-gather(bf16[1,48,256]{2,1,0:T(8,128)(2,1)S(1)} %copy-done.30), channel_id=1, replica_groups=mesh['leaf'=8,'seq'=4] {'seq'}, dimensions={1}, use_global_device_ids=true | all-gather | bytes 122880 | tf_op jit(solution)/shard_map/all_gather | solution.py:80
  38.2 14.4 %all_gather.18 = bf16[1,192,256]{2,1,0:T(8,128)(2,1)S(1)} all-gather(bf16[1,48,256]{2,1,0:T(8,128)(2,1)S(1)} %copy-done.31), channel_id=1, replica_groups=mesh['leaf'=8,'seq'=4] {'seq'}, dimensions={1}, use_global_device_ids=true | all-gather | bytes 122880 | tf_op jit(solution)/shard_map/all_gather | solution.py:81
  52.7 18.1 %all_gather.15 = bf16[1,512,256]{2,1,0:T(8,128)(2,1)S(1)} all-gather(bf16[1,128,256]{2,1,0:T(8,128)(2,1)S(1)} %copy-done.28), channel_id=1, replica_groups=mesh['leaf'=8,'seq'=4] {'seq'}, dimensions={1}, use_global_device_ids=true | all-gather | bytes 327680 | tf_op jit(solution)/shard_map/all_gather | solution.py:78
  70.8 17.8 %all_gather.17 = bf16[1,512,256]{2,1,0:T(8,128)(2,1)S(1)} all-gather(bf16[1,128,256]{2,1,0:T(8,128)(2,1)S(1)} %copy-done.29), channel_id=1, replica_groups=mesh['leaf'=8,'seq'=4] {'seq'}, dimensions={1}, use_global_device_ids=true | all-gather | bytes 327680 | tf_op jit(solution)/shard_map/all_gather | solution.py:79
  89.0 3.3 %fusion.76 = (f32[7,176]{1,0:T(8,128)S(1)}, f32[7,176,704]{2,1,0:T(8,128)}) fusion(pred[176,704]{1,0:T(8,128)(4,1)S(1)} %pad_add_fusion, bf16[192,256]{1,0:T(8,128)(2,1)S(1)} %bitcast.199, bf16[512,256]{1,0:T(8,128)(2,1)S(1)} %bitcast.185, bf16[48,2,7,128]{3,0,2,1:T(8,128)(2,1)S(1)} %copy-done.24, bf16[128,2,7,128]{3,0,2,1:T(8,128)(2,1)S(1)} %copy-done.20), kind=kOutput, calls=%fused_computation.103 | convolution fusion | flops 226497216 | bytes 4589376 | tf_op jit(solution)/shard_map/sub | solution.py:120
  92.4 2.4 %fusion.17 = bf16[7,176,704]{2,1,0:T(8,128)(2,1)S(1)} fusion(f32[7,176,704]{2,1,0:T(8,128)} %get-tuple-element.38, f32[7,176]{1,0:T(8,128)S(1)} %get-tuple-element.37), kind=kLoop, calls=%fused_computation.27 | loop fusion | flops 1734656 | bytes 5208896 | tf_op jit(solution)/shard_map/convert_element_type | solution.py:122
  94.8 2.0 multiply_reduce_fusion
  96.8 4.4 %fusion.67 = (f32[7,176]{1,0:T(8,128)S(1)}, f32[7,176,704]{2,1,0:T(8,128)}) fusion(pred[176,704]{1,0:T(8,128)(4,1)} %copy-done.27, bf16[512,256]{1,0:T(8,128)(2,1)S(1)} %bitcast.186, bf16[192,256]{1,0:T(8,128)(2,1)S(1)} %bitcast.200, bf16[128,2,7,128]{3,0,2,1:T(8,128)(2,1)} %copy.41, bf16[48,2,7,128]{3,0,2,1:T(8,128)(2,1)S(1)} %copy-done.25), kind=kOutput, calls=%fused_computation.102 | convolution fusion | flops 226497216 | bytes 4589376 | tf_op jit(solution)/shard_map/sub | solution.py:120
  101.3 2.4 %fusion.16 = bf16[7,176,704]{2,1,0:T(8,128)(2,1)S(1)} fusion(f32[7,176,704]{2,1,0:T(8,128)} %get-tuple-element.34, f32[7,176]{1,0:T(8,128)S(1)} %get-tuple-element.33), kind=kLoop, calls=%fused_computation.26 | loop fusion | flops 1734656 | bytes 5208896 | tf_op jit(solution)/shard_map/convert_element_type | solution.py:122
  103.7 1.2 copy-done
  104.9 1.4 multiply_reduce_fusion.1
  106.8 1.1 pad_maximum_fusion.1
  107.9 5.4 %all-to-all-start = ((bf16[4,176,8,1,56]{1,4,2,3,0:T(8,128)(2,1)}), bf16[4,176,8,1,56]{1,4,2,3,0:T(8,128)(2,1)S(1)}, u32[]{:S(2)}, u32[]{:S(2)}) async-start(bf16[4,176,8,1,56]{1,4,2,3,0:T(8,128)(2,1)} %pad_maximum_fusion.1), calls=%async_computation.1 | async-start | bytes 1835008 | tf_op jit(solution)/shard_map/all_to_all | solution.py:40
  113.4 2.7 %fusion.4 = bf16[7,176,704]{2,1,0:T(8,128)(2,1)S(1)} fusion(f32[7,176]{1,0:T(8,128)S(1)} %bitcast.211, f32[7,176,704]{2,1,0:T(8,128)} %get-tuple-element.38, f32[7,176]{1,0:T(8,128)S(1)} %get-tuple-element.37, bf16[176,1,7,128]{3,2,1,0:T(8,128)(2,1)S(1)} %copy-done.14, bf16[192,256]{1,0:T(8,128)(2,1)} %bitcast.205, bf16[512,256]{1,0:T(8,128)(2,1)S(1)} %bitcast.191), kind=kOutput, calls=%fused_computation.6 | convolution fusion | flops 226733056 | bytes 5889664 | tf_op jit(solution)/shard_map/qhd,kd->hqk/dot_general | solution.py:140
  116.2 1.3 copy-done.7
  117.5 0.7 convolution_bitcast_fusion.4
  120.4 1.1 fusion.7
  121.5 0.7 convolution_bitcast_fusion.5
  122.8 0.9 pad_maximum_fusion.2
  123.8 22.1 %all-to-all-done = bf16[4,176,8,1,56]{1,4,2,3,0:T(8,128)(2,1)S(1)} async-done(((bf16[4,176,8,1,56]{1,4,2,3,0:T(8,128)(2,1)}), bf16[4,176,8,1,56]{1,4,2,3,0:T(8,128)(2,1)S(1)}, u32[]{:S(2)}, u32[]{:S(2)}) %all-to-all-start) | async-done | bytes 630816 | tf_op jit(solution)/shard_map/all_to_all | solution.py:40
  146.6 0.7 reshape_reshape.7
  147.4 6.5 %convolution_convert_fusion = bf16[448,3584]{1,0:T(8,128)(2,1)} fusion(bf16[704,448]{0,1:T(8,128)(2,1)S(1)} %reshape_reshape.7, bf16[704,3584]{1,0:T(8,128)(2,1)} %all-gather.2.cloned.1.call-done), kind=kOutput, calls=%fused_computation.2 | convolution fusion | flops 2262335488 | bytes 8888320 | tf_op jit(solution)/shard_map/dot_general | solution.py:45
  153.9 0.9 copy-done.4
  156.2 0.9 copy-done.10
  158.1 1.2 copy.52
  159.5 0.8 broadcast_in_dim.33
  160.3 1.0 convert_element_type.75
  162.6 38.8 %reduce-scatter.5.cloned.1.call-done = bf16[56,3584]{1,0:T(8,128)(2,1)} async-done(((bf16[448,3584]{1,0:T(8,128)(2,1)}), bf16[56,3584]{1,0:T(8,128)(2,1)}) %reduce-scatter.5.cloned.1.call-update) | async-done | bytes 401424 | tf_op jit(solution)/shard_map/reduce_scatter | solution.py:48
  201.5 1.9 convert_multiply_fusion
  (113 shorter events, 10.9 us)
Async XLA Ops:
  7.2 2.6 %copy-start.34 = (s32[1,16]{1,0:T(1,128)S(1)}, s32[1,16]{1,0:T(1,128)}, u32[]{:S(2)}) copy-start(s32[1,16]{1,0:T(1,128)} %param.21) | copy-start | bytes 196
  7.2 3.0 %copy-start.36 = (s32[1,16]{1,0:T(1,128)S(1)}, s32[1,16]{1,0:T(1,128)}, u32[]{:S(2)}) copy-start(s32[1,16]{1,0:T(1,128)} %param.23) | copy-start | bytes 196
  7.2 3.0 %copy-start.35 = (s32[1,16]{1,0:T(1,128)S(1)}, s32[1,16]{1,0:T(1,128)}, u32[]{:S(2)}) copy-start(s32[1,16]{1,0:T(1,128)} %param.22) | copy-start | bytes 196
  7.2 3.1 %copy-start.23 = (bf16[1,48,1792]{2,1,0:T(8,128)(2,1)S(1)}, bf16[1,48,1792]{2,1,0:T(8,128)(2,1)}, u32[]{:S(2)}) copy-start(bf16[1,48,1792]{2,1,0:T(8,128)(2,1)} %param.15) | copy-start | bytes 516100
  7.2 4.0 %copy-start.19 = (bf16[1,128,1792]{2,1,0:T(8,128)(2,1)S(1)}, bf16[1,128,1792]{2,1,0:T(8,128)(2,1)}, u32[]{:S(2)}) copy-start(bf16[1,128,1792]{2,1,0:T(8,128)(2,1)} %param.12) | copy-start | bytes 1376260
  7.2 140.2 %all-gather.2.cloned.1.call-start = ((), (), s32[]{:S(2)}) async-start(), calls=%async_computation.4 | async-start | bytes 6307840 | tf_op jit(solution)/shard_map/all_gather | solution.py:44
  9.8 2.7 %copy-start.16 = (bf16[1,128,3584]{2,1,0:T(8,128)(2,1)S(1)}, bf16[1,128,3584]{2,1,0:T(8,128)(2,1)}, u32[]{:S(2)}) copy-start(bf16[1,128,3584]{2,1,0:T(8,128)(2,1)} %param.18) | copy-start | bytes 2752516
  9.8 2.7 %copy-start.22 = (bf16[1,48,3584]{2,1,0:T(8,128)(2,1)S(1)}, bf16[1,48,3584]{2,1,0:T(8,128)(2,1)}, u32[]{:S(2)}) copy-start(bf16[1,48,3584]{2,1,0:T(8,128)(2,1)} %param.19) | copy-start | bytes 1032196
  12.5 9.8 %copy-start.30 = (bf16[1,48,256]{2,1,0:T(8,128)(2,1)S(1)}, bf16[1,48,256]{2,1,0:T(8,128)(2,1)}, u32[]{:S(2)}) copy-start(bf16[1,48,256]{2,1,0:T(8,128)(2,1)} %param.16) | copy-start | bytes 73732
  12.5 25.8 %copy-start.31 = (bf16[1,48,256]{2,1,0:T(8,128)(2,1)S(1)}, bf16[1,48,256]{2,1,0:T(8,128)(2,1)}, u32[]{:S(2)}) copy-start(bf16[1,48,256]{2,1,0:T(8,128)(2,1)} %param.17) | copy-start | bytes 73732
  12.5 40.2 %copy-start.28 = (bf16[1,128,256]{2,1,0:T(8,128)(2,1)S(1)}, bf16[1,128,256]{2,1,0:T(8,128)(2,1)}, u32[]{:S(2)}) copy-start(bf16[1,128,256]{2,1,0:T(8,128)(2,1)} %param.13) | copy-start | bytes 196612
  12.5 58.3 %copy-start.29 = (bf16[1,128,256]{2,1,0:T(8,128)(2,1)S(1)}, bf16[1,128,256]{2,1,0:T(8,128)(2,1)}, u32[]{:S(2)}) copy-start(bf16[1,128,256]{2,1,0:T(8,128)(2,1)} %param.14) | copy-start | bytes 196612
  21.5 67.5 %copy-start.20 = (bf16[128,2,7,128]{3,0,2,1:T(8,128)(2,1)S(1)}, bf16[128,2,7,128]{3,0,2,1:T(8,128)(2,1)}, u32[]{:S(2)}) copy-start(bf16[128,2,7,128]{3,0,2,1:T(8,128)(2,1)} %copy.41) | copy-start | bytes 1376260
  21.5 67.5 %copy-start.24 = (bf16[48,2,7,128]{3,0,2,1:T(8,128)(2,1)S(1)}, bf16[48,2,7,128]{3,0,2,1:T(8,128)(2,1)}, u32[]{:S(2)}) copy-start(bf16[48,2,7,128]{3,0,2,1:T(8,128)(2,1)} %copy.42) | copy-start | bytes 516100
  52.7 51.0 %copy-start.17 = (bf16[1,192,256]{2,1,0:T(8,128)(2,1)}, bf16[1,192,256]{2,1,0:T(8,128)(2,1)S(1)}, u32[]{:S(2)}) copy-start(bf16[1,192,256]{2,1,0:T(8,128)(2,1)S(1)} %all_gather.18) | copy-start | bytes 294916
  70.8 26.1 %copy-start.3 = (bf16[1,512,256]{2,1,0:T(8,128)(2,1)}, bf16[1,512,256]{2,1,0:T(8,128)(2,1)S(1)}, u32[]{:S(2)}) copy-start(bf16[1,512,256]{2,1,0:T(8,128)(2,1)S(1)} %all_gather.15) | copy-start | bytes 786436
  88.5 15.1 %copy-start.5 = (bf16[1,512,256]{2,1,0:T(8,128)(2,1)}, bf16[1,512,256]{2,1,0:T(8,128)(2,1)S(1)}, u32[]{:S(2)}) copy-start(bf16[1,512,256]{2,1,0:T(8,128)(2,1)S(1)} %all_gather.17) | copy-start | bytes 786436
  88.9 3.4 %copy-start.27 = (pred[176,704]{1,0:T(8,128)(4,1)}, pred[176,704]{1,0:T(8,128)(4,1)S(1)}, u32[]{:S(2)}) copy-start(pred[176,704]{1,0:T(8,128)(4,1)S(1)} %pad_add_fusion) | copy-start | bytes 371716
  89.0 5.8 %copy-start.13 = (bf16[176,1,7,128]{3,2,1,0:T(8,128)(2,1)}, bf16[176,1,7,128]{3,2,1,0:T(8,128)(2,1)S(1)}, u32[]{:S(2)}) copy-start(bf16[176,1,7,128]{3,2,1,0:T(8,128)(2,1)S(1)} %get-tuple-element.27) | copy-start | bytes 946180
  89.0 14.7 %copy-start.11 = (bf16[176,1,7,128]{3,2,1,0:T(8,128)(2,1)}, bf16[176,1,7,128]{3,2,1,0:T(8,128)(2,1)S(1)}, u32[]{:S(2)}) copy-start(bf16[176,1,7,128]{3,2,1,0:T(8,128)(2,1)S(1)} %get-tuple-element.28) | copy-start | bytes 946180
  103.6 2.7 %copy-start.15 = (bf16[128,7,176]{0,2,1:T(8,128)(2,1)S(1)}, bf16[128,7,176]{0,2,1:T(8,128)(2,1)}, u32[]{:S(2)}) copy-start(bf16[128,7,176]{0,2,1:T(8,128)(2,1)} %get-tuple-element.40) | copy-start | bytes 946180
  106.7 6.7 %copy-start.6 = (bf16[1,512,256]{2,1,0:T(8,128)(2,1)S(1)}, bf16[1,512,256]{2,1,0:T(8,128)(2,1)}, u32[]{:S(2)}) copy-start(bf16[1,512,256]{2,1,0:T(8,128)(2,1)} %copy-done.5) | copy-start | bytes 786436
  106.7 6.7 %copy-start.14 = (bf16[176,1,7,128]{3,2,1,0:T(8,128)(2,1)S(1)}, bf16[176,1,7,128]{3,2,1,0:T(8,128)(2,1)}, u32[]{:S(2)}) copy-start(bf16[176,1,7,128]{3,2,1,0:T(8,128)(2,1)} %copy-done.13) | copy-start | bytes 946180
  106.7 6.7 %copy-start.33 = (f32[176,7]{0,1:T(8,128)S(1)}, f32[176,7]{0,1:T(8,128)}, u32[]{:S(2)}) copy-start(f32[176,7]{0,1:T(8,128)} %get-tuple-element.39) | copy-start | bytes 14788
  107.9 38.0 %all-to-all-start = ((bf16[4,176,8,1,56]{1,4,2,3,0:T(8,128)(2,1)}), bf16[4,176,8,1,56]{1,4,2,3,0:T(8,128)(2,1)S(1)}, u32[]{:S(2)}, u32[]{:S(2)}) async-start(bf16[4,176,8,1,56]{1,4,2,3,0:T(8,128)(2,1)} %pad_maximum_fusion.1), calls=%async_computation.1 | async-start | bytes 1835008 | tf_op jit(solution)/shard_map/all_to_all | solution.py:40
  113.4 46.9 %reduce-scatter.3.cloned.1.call-start = ((), (), s32[]{:S(2)}) async-start(), calls=%async_computation.3 | async-start | bytes 901120 | tf_op jit(solution)/shard_map/reduce_scatter | solution.py:199
  113.4 4.1 %copy-start.21 = (bf16[128,2,7,128]{3,0,2,1:T(8,128)(2,1)S(1)}, bf16[128,2,7,128]{3,0,2,1:T(8,128)(2,1)}, u32[]{:S(2)}) copy-start(bf16[128,2,7,128]{3,0,2,1:T(8,128)(2,1)} %copy.41) | copy-start | bytes 1376260
  113.4 4.0 %copy-start.26 = (bf16[48,2,7,128]{3,0,2,1:T(8,128)(2,1)S(1)}, bf16[48,2,7,128]{3,0,2,1:T(8,128)(2,1)}, u32[]{:S(2)}) copy-start(bf16[48,2,7,128]{3,0,2,1:T(8,128)(2,1)} %copy.42) | copy-start | bytes 516100
  118.2 2.2 %copy-start.2 = (f32[7,176,704]{2,1,0:T(8,128)S(1)}, f32[7,176,704]{2,1,0:T(8,128)}, u32[]{:S(2)}) copy-start(f32[7,176,704]{2,1,0:T(8,128)} %get-tuple-element.34) | copy-start | bytes 10407940
  118.2 2.2 %copy-start.18 = (bf16[1,192,256]{2,1,0:T(8,128)(2,1)S(1)}, bf16[1,192,256]{2,1,0:T(8,128)(2,1)}, u32[]{:S(2)}) copy-start(bf16[1,192,256]{2,1,0:T(8,128)(2,1)} %copy-done.17) | copy-start | bytes 294916
  118.2 2.2 %copy-start.32 = (f32[176,7]{0,1:T(8,128)S(1)}, f32[176,7]{0,1:T(8,128)}, u32[]{:S(2)}) copy-start(f32[176,7]{0,1:T(8,128)} %get-tuple-element.35) | copy-start | bytes 14788
  123.8 77.7 %reduce-scatter.5.cloned.1.call-start = ((), (), s32[]{:S(2)}) async-start(), calls=%async_computation.5 | async-start | bytes 3612672 | tf_op jit(solution)/shard_map/reduce_scatter | solution.py:48
  (9 other events, 13.0 us)
Sparse Core Ops, SparseCore 0:
  9.9 114.9 all-gather.1
  127.8 22.9 reduce-scatter.2
  154.2 47.2 reduce-scatter.4
